TPU v7x, 512 devices: a whole 4x4x16 slice. The times are simulated.
512 devices in a mesh: grp: 16 (over y, x), sp: 32 (over z, core).
Axes of the slice: x: 4, y: 4, z: 16, core: 2. Of those that a mesh axis runs over, the one named last changes fastest.
Arguments:
- coarse: bfloat16 [1024, 48, 1024], P(('grp', 'sp')), parts along dimension 0, may hold values from -30 to 30
- conv_weight: bfloat16 [1024, 3, 3, 1024], P('sp'), may hold values from -0.104166667 to 0.104166667
- conv_bias: float32 [1024], P('sp'), may hold values from -5 to 5
- norm_gain: float32 [1024], P('sp'), may hold values from 0.5 to 1.5
- norm_shift: float32 [1024], P('sp'), may hold values from -3 to 3
- up_weight: bfloat16 [512, 2, 2, 1024], P('sp'), may hold values from -0.1875 to 0.1875
- up_bias: bfloat16 [512], P('sp'), may hold values from -3 to 3
Outputs:
- fine: bfloat16 [2048, 96, 512], P(('grp', 'sp')), parts along dimension 0
There are 16 independent parts, one for each index of `grp`. A program takes and returns all parts, laid end to end along the dimension named above; an argument that names none is the same for every part. Nothing has to cross between parts.
All inputs are finite; a program needn't handle non-finite values.
Results may differ from a plain program's by a relative error of at most 0.0042.
Values may be sent and summed in bfloat16 or wider, within the bound.
No kernel may reach another device: no remote copies, remote signals or barrier semaphores. Data moves between devices by JAX's collectives and lax.ppermute only.
A program may use at most 64 MiB of HBM per device.

v0:
```python
import jax
import jax.numpy as jnp
from jax import lax
from jax.sharding import PartitionSpec as P

GSIZE = 32


def conv_rows(weights_cat, width_cols, channels, outputs, tile_rows):
    how_many = tile_rows.shape[0]
    padded = jnp.pad(tile_rows, ((0, 0), (1, 1), (0, 0)))
    partial_sum = jnp.zeros((how_many * width_cols, 3 * outputs), jnp.float32)
    for offset in range(3):
        window = padded[:, offset : offset + width_cols, :].reshape(how_many * width_cols, channels)
        partial_sum = partial_sum + jnp.dot(
            window, weights_cat[offset], preferred_element_type=jnp.float32
        )
    partial_sum = partial_sum.reshape(how_many, width_cols, 3, outputs)
    contrib = jnp.zeros((how_many + 2, width_cols, outputs), jnp.float32)
    for kernel_row in range(3):
        contrib = contrib.at[2 - kernel_row : 2 - kernel_row + how_many].add(
            partial_sum[:, :, kernel_row]
        )
    return contrib


def normalize(convolved, height, width_cols, outputs, norm_gain, norm_shift):
    grouped = convolved.reshape(height, width_cols, outputs // GSIZE, GSIZE)
    centre = jnp.mean(grouped, axis=(0, 1, 3), keepdims=True)
    spread = jnp.mean(jnp.square(grouped - centre), axis=(0, 1, 3), keepdims=True)
    normed = ((grouped - centre) * lax.rsqrt(spread + 1e-05)).reshape(height, width_cols, outputs)
    return jax.nn.silu(normed * norm_gain + norm_shift).astype(jnp.bfloat16)


def full_conv(coarse, conv_weight, conv_bias, norm_gain, norm_shift):
    tile_count = lax.axis_size("sp")
    local_rows, width_cols, channels = coarse.shape
    height = local_rows * tile_count
    outputs = conv_weight.shape[0]
    weights_cat = jnp.transpose(conv_weight, (2, 3, 1, 0)).reshape(3, channels, 3 * outputs)
    summed = conv_rows(
        weights_cat, width_cols, channels, outputs, lax.all_gather(coarse, "sp", axis=0, tiled=True)
    )
    convolved = summed[1 : height + 1] + conv_bias
    return normalize(convolved, height, width_cols, outputs, norm_gain, norm_shift)


def body(coarse, conv_weight, conv_bias, norm_gain, norm_shift, up_weight, up_bias):
    activated = full_conv(coarse, conv_weight, conv_bias, norm_gain, norm_shift)
    height, width_cols, channels = (activated.shape[0], activated.shape[1], conv_weight.shape[3])
    slice_out = up_weight.shape[0]
    flat_weight = jnp.transpose(up_weight, (3, 1, 2, 0)).reshape(channels, 4 * slice_out)
    features = lax.all_gather(activated, "sp", axis=2, tiled=True)
    chosen_width = features.shape[2]
    flat_features = features.reshape(height * width_cols, chosen_width)
    decoded = jnp.dot(flat_features, flat_weight, preferred_element_type=jnp.float32)
    decoded = (decoded.reshape(height, width_cols, 2, 2, slice_out) + up_bias).astype(jnp.bfloat16)
    decoded = jnp.transpose(decoded, (0, 2, 1, 3, 4)).reshape(2 * height, 2 * width_cols, slice_out)
    return lax.all_to_all(decoded, "sp", split_axis=0, concat_axis=2, tiled=True)


def solution(mesh):
    return jax.shard_map(
        body,
        mesh=mesh,
        in_specs=(
            P(("grp", "sp"), None, None),
            P("sp", None, None, None),
            P("sp"),
            P("sp"),
            P("sp"),
            P("sp", None, None, None),
            P("sp"),
        ),
        out_specs=P(("grp", "sp"), None, None),
        check_vma=False,
    )
```

profile of v0, /device:TPU:1, one launch (start us, length us, event | category | flops | bytes accessed | tf_op | source)
XLA Modules:
  0.0 294.0 jit_solution(15745474738051141578)
XLA Ops:
  6.5 0.7 all-gather.3.cloned.1.call-update
  7.3 0.0 all-gather.5.cloned.1.call-start
  7.3 1.2 fusion.14
  8.5 83.6 %all-gather.3.cloned.1.call-done = bf16[64,48,1024]{2,1,0:T(8,128)(2,1)} async-done(((bf16[2,48,1024]{2,1,0:T(8,128)(2,1)}), bf16[64,48,1024]{2,1,0:T(8,128)(2,1)}) %all-gather.3.cloned.1.call-update) | async-done | bytes 6291472 | tf_op jit(solution)/shard_map/all_gather | solution.py:42
  92.1 10.7 %pad_slice_fusion = (bf16[64,48,1024]{2,1,0:T(8,128)(2,1)S(1)}, bf16[64,48,1024]{2,1,0:T(8,128)(2,1)S(1)}) fusion(bf16[64,48,1024]{2,1,0:T(8,128)(2,1)} %all-gather.3.cloned.1.call-done), kind=kLoop, calls=%fused_computation.2 | loop fusion | bytes 18874368 | tf_op jit(solution)/shard_map/slice | solution.py:14
  102.9 2.0 fusion.15
  104.9 0.7 copy-done
  105.7 2.0 convolution_add_fusion.1
  107.7 3.1 %convolution_add_fusion = f32[3072,96]{0,1:T(8,128)} fusion(f32[3072,96]{0,1:T(8,128)S(1)} %convolution_add_fusion.1, bf16[3072,1024]{1,0:T(8,128)(2,1)S(1)} %bitcast.56, bf16[1024,96]{0,1:T(8,128)(2,1)S(1)} %bitcast.62), kind=kOutput, calls=%fused_computation.4 | convolution fusion | flops 604274688 | bytes 8847360 | tf_op jit(solution)/shard_map/dot_general | solution.py:15
  110.8 2.6 reshape.152
  113.4 0.2 fusion.13
  113.7 0.6 copy.44
  114.3 0.1 scatter-add.10
  114.4 1.0 fusion.9
  115.4 1.0 fusion.7
  116.4 1.0 fusion.10
  118.0 0.9 multiply_reduce_fusion
  119.7 1.3 multiply_convert_fusion
  121.0 104.1 %all-gather.5.cloned.1.call-done = bf16[64,48,1024]{1,2,0:T(8,128)(2,1)} async-done(((bf16[64,48,32]{1,2,0:T(8,128)(2,1)}), bf16[64,48,1024]{1,2,0:T(8,128)(2,1)}) %all-gather.5.cloned.1.call-update) | async-done | bytes 6291472 | tf_op jit(solution)/shard_map/all_gather | solution.py:53
  225.1 9.7 %fusion.4 = bf16[64,2,48,2,16]{2,4,3,1,0:T(8,128)(2,1)} fusion(bf16[64,48,1024]{1,2,0:T(8,128)(2,1)} %all-gather.5.cloned.1.call-done, f32[16]{0:T(128)S(1)} %convert_element_type.16, bf16[16,2,2,1024]{3,2,1,0:T(2,128)(2,1)S(1)} %copy-done.1), kind=kOutput, calls=%fused_computation.7 | convolution fusion | flops 403046400 | bytes 6815808 | tf_op jit(solution)/shard_map/dot_general | solution.py:56
  234.8 6.1 %copy.23 = bf16[64,2,48,2,16]{4,3,2,1,0:T(2,128)(2,1)S(1)} copy(bf16[64,2,48,2,16]{2,4,3,1,0:T(8,128)(2,1)} %fusion.4) | data formatting | bytes 786432 | tf_op jit(solution)/shard_map/convert_element_type | solution.py:57
  240.9 2.7 copy.24
  243.5 42.6 %all_to_all.18 = bf16[128,96,16]{1,2,0:T(8,128)(2,1)S(1)} all-to-all(bf16[128,96,16]{1,2,0:T(8,128)(2,1)} %copy.24), channel_id=1, replica_groups=mesh['grp'=16,'sp'=32] {'sp'}, dimensions={0} | all-to-all | bytes 786432 | tf_op jit(solution)/shard_map/all_to_all | solution.py:59
  286.2 1.0 copy.26
  (15 shorter events, 0.1 us)
Async XLA Ops:
  6.5 85.6 %all-gather.3.cloned.1.call-start = ((), (), s32[]{:S(2)}) async-start(), calls=%async_computation.1 | async-start | bytes 6488064 | tf_op jit(solution)/shard_map/all_gather | solution.py:42
  7.3 217.8 %all-gather.5.cloned.1.call-start = ((), (), s32[]{:S(2)}) async-start(), calls=%async_computation.2 | async-start | bytes 17301504 | tf_op jit(solution)/shard_map/all_gather | solution.py:53
  102.9 2.8 copy-start
  114.4 2.0 copy-start.2
  115.4 4.3 %copy-start.3 = (f32[32]{0:T(128)S(1)}, f32[32]{0:T(128)}, u32[]{:S(2)}) copy-start(f32[32]{0:T(128)} %param.17) | copy-start | bytes 388
  115.4 4.3 %copy-start.4 = (f32[32]{0:T(128)S(1)}, f32[32]{0:T(128)}, u32[]{:S(2)}) copy-start(f32[32]{0:T(128)} %param.16) | copy-start | bytes 388
  115.4 5.6 %copy-start.5 = (bf16[16]{0:T(256)(128)(2,1)S(1)}, bf16[16]{0:T(256)(128)(2,1)}, u32[]{:S(2)}) copy-start(bf16[16]{0:T(256)(128)(2,1)} %param.19) | copy-start | bytes 100
  115.4 109.6 %copy-start.1 = (bf16[16,2,2,1024]{3,2,1,0:T(2,128)(2,1)S(1)}, bf16[16,2,2,1024]{3,2,1,0:T(2,128)(2,1)}, u32[]{:S(2)}) copy-start(bf16[16,2,2,1024]{3,2,1,0:T(2,128)(2,1)} %param.18) | copy-start | bytes 393220
Sparse Core Ops, SparseCore 0:
  9.5 82.6 all-gather.2
  121.1 103.9 all-gather.4
where the time goes:
time: 294 us
  waiting for transfers between devices  188 us (64%)
  blocking collectives  42.6 us (14%)
  local copies, waits for them, and re-layouts  26 us (9%)
  matrix products  16.9 us (6%)
  between operations  14.9 us (5%)
  other arithmetic  5.12 us (2%)
    all_gather x1, waiting for transfers between devices, body(): features = lax.all_gather(activated, 'sp', axis=2, tiled=True)  104 us
    all_gather x1, waiting for transfers between devices, full_conv(): lax.all_gather(coarse, 'sp', axis=0, tiled=True)  83.6 us
    all_to_all x1, blocking collectives, body(): lax.all_to_all(decoded, 'sp', split_axis=0, concat_axis=2, tiled=True)  42.6 us
    slice x1, local copies, waits for them, and re-layouts, conv_rows(): padded[:, offset:offset + width_cols, :]  10.7 us
    dot_general x1, matrix products, body(): jnp.dot(flat_features, flat_weight, preferred_element_type=jnp.float32)  9.72 us
    dot_general x3, matrix products, conv_rows(): jnp.dot(window, weights_cat[offset], preferred_element_type=jnp.float32)  7.18 us
    convert_element_type x1, local copies, waits for them, and re-layouts, body(): (decoded.reshape(height, width_cols, 2, 2, slice_out) + up_bias).astype(j...  6.09 us
  transfers between devices with their start and end apart: 2, of which 2 were waited for; matrix products, arithmetic and copies ran while one was open for 0% of the time, Pallas kernels for 0%

commit v1 on v0

--- a/solution.py
+++ b/solution.py
@@ -4,6 +4,13 @@
 from jax.sharding import PartitionSpec as P
 
 GSIZE = 32
+
+
+def swapped_in(x, axis, along):
+    n_dev = lax.axis_size(axis)
+    blocks = jnp.stack([x for _ in range(n_dev)])
+    blocks = lax.all_to_all(blocks, axis, split_axis=0, concat_axis=0)
+    return jnp.concatenate(blocks, axis=along)
 
 
 def conv_rows(weights_cat, width_cols, channels, outputs, tile_rows):
@@ -50,7 +57,7 @@
     height, width_cols, channels = (activated.shape[0], activated.shape[1], conv_weight.shape[3])
     slice_out = up_weight.shape[0]
     flat_weight = jnp.transpose(up_weight, (3, 1, 2, 0)).reshape(channels, 4 * slice_out)
-    features = lax.all_gather(activated, "sp", axis=2, tiled=True)
+    features = swapped_in(activated, "sp", 2)
     chosen_width = features.shape[2]
     flat_features = features.reshape(height * width_cols, chosen_width)
     decoded = jnp.dot(flat_features, flat_weight, preferred_element_type=jnp.float32)

time: 294 us -> 539 us (1.83)
  waiting for transfers between devices: 188 us -> 359 us
  local copies, waits for them, and re-layouts: 26 us -> 96.1 us
  starting transfers between devices: 0.04 us -> 8.58 us
  matrix products: 16.9 us -> 10.3 us
    all_to_all x0 -> x1, waiting for transfers between devices: none -> 275 us  [swapped_in(): blocks = lax.all_to_all(blocks, axis, split_axis=0, concat_axis=0)]
    all_gather x1 -> x0, waiting for transfers between devices: 104 us -> none  [body(): features = lax.all_gather(activated, 'sp', axis=2, tiled=True)]
    unnamed x13 -> x17, local copies, waits for them, and re-layouts: 1.37 us -> 57.3 us
    reshape x0 -> x2, local copies, waits for them, and re-layouts: none -> 8.73 us  [swapped_in(): return jnp.concatenate(blocks, axis=along)]
    all_to_all x0 -> x1, starting transfers between devices: none -> 8.58 us  [swapped_in(): blocks = lax.all_to_all(blocks, axis, split_axis=0, concat_axis=0)]
    dot_general x1, matrix products: 9.72 us -> 3.14 us  [body(): jnp.dot(flat_features, flat_weight, preferred_element_type=jnp.float32)]
where the time goes in v1:
time: 539 us; the launch traced here: 537 us
  waiting for transfers between devices  359 us (67%)
  local copies, waits for them, and re-layouts  96.1 us (18%)
  blocking collectives  42.3 us (8%)
  between operations  14.9 us (3%)
  matrix products  10.3 us (2%)
  starting transfers between devices  8.58 us (2%)
    all_to_all x1, waiting for transfers between devices, swapped_in(): blocks = lax.all_to_all(blocks, axis, split_axis=0, concat_axis=0)  275 us
    all_gather x1, waiting for transfers between devices, full_conv(): lax.all_gather(coarse, 'sp', axis=0, tiled=True)  83.7 us
    unnamed x17, local copies, waits for them, and re-layouts  57.3 us
    all_to_all x1, blocking collectives, body(): lax.all_to_all(decoded, 'sp', split_axis=0, concat_axis=2, tiled=True)  42.3 us
  transfers between devices with their start and end apart: 2, of which 2 were waited for; matrix products, arithmetic and copies ran while one was open for 0% of the time, Pallas kernels for 0%

profile of v1, /device:TPU:1, one launch (start us, length us, event | category | flops | bytes accessed | tf_op | source)
XLA Modules:
  0.0 536.7 jit_solution(13708723689854922937)
XLA Ops:
  7.3 1.2 fusion.7
  8.4 83.7 %all-gather.2.cloned.1.call-done = bf16[64,48,1024]{2,1,0:T(8,128)(2,1)} async-done(((bf16[2,48,1024]{2,1,0:T(8,128)(2,1)}), bf16[64,48,1024]{2,1,0:T(8,128)(2,1)}) %all-gather.2.cloned.1.call-update) | async-done | bytes 6291472 | tf_op jit(solution)/shard_map/all_gather | solution.py:49
  92.1 10.7 %pad_slice_fusion = (bf16[64,48,1024]{2,1,0:T(8,128)(2,1)S(1)}, bf16[64,48,1024]{2,1,0:T(8,128)(2,1)S(1)}) fusion(bf16[64,48,1024]{2,1,0:T(8,128)(2,1)} %all-gather.2.cloned.1.call-done), kind=kLoop, calls=%fused_computation | loop fusion | bytes 18874368 | tf_op jit(solution)/shard_map/slice | solution.py:21
  102.9 2.0 fusion.8
  105.7 2.0 convolution_add_fusion.1
  107.7 3.1 convolution_add_fusion
  110.8 2.4 reshape.157
  113.4 1.5 copy-done.1
  114.9 1.2 fusion.3
  116.3 5.2 scatter-add.11
  121.5 1.5 fusion.2
  123.0 1.0 fusion.4
  124.6 1.0 multiply_reduce_fusion
  127.6 7.4 %broadcast_bitcast_fusion = bf16[32,48,32,64]{3,2,1,0:T(8,128)(2,1)} fusion(bf16[64,48,32]{0,2,1:T(8,128)(2,1)S(1)} %copy.16), kind=kLoop, calls=%fused_computation.20 | loop fusion | bytes 6488064
  134.9 24.2 %reshape.165 = bf16[32,2,49152]{2,1,0:T(2,128)(2,1)} reshape(bf16[32,48,32,64]{3,2,1,0:T(8,128)(2,1)} %broadcast_bitcast_fusion) | data formatting | bytes 12582912
  159.1 8.6 %all-to-all-start = ((bf16[32,2,49152]{2,1,0:T(2,128)(2,1)}), bf16[32,2,49152]{2,1,0:T(2,128)(2,1)}, u32[]{:S(2)}, u32[]{:S(2)}) async-start(bf16[32,2,49152]{2,1,0:T(2,128)(2,1)} %reshape.165), calls=%async_computation | async-start | bytes 12582912 | tf_op jit(solution)/shard_map/all_to_all | solution.py:12
  167.7 274.7 %all-to-all-done = bf16[32,2,49152]{2,1,0:T(2,128)(2,1)} async-done(((bf16[32,2,49152]{2,1,0:T(2,128)(2,1)}), bf16[32,2,49152]{2,1,0:T(2,128)(2,1)}, u32[]{:S(2)}, u32[]{:S(2)}) %all-to-all-start) | async-done | bytes 6291488 | tf_op jit(solution)/shard_map/all_to_all | solution.py:12
  442.4 23.4 %reshape.166 = bf16[32,48,32,64]{3,2,1,0:T(8,128)(2,1)} reshape(bf16[32,2,49152]{2,1,0:T(2,128)(2,1)} %all-to-all-done) | data formatting | bytes 12582912
  465.9 7.2 %bitcast_bitcast_fusion = bf16[64,48,32,32]{0,3,1,2:T(8,128)(2,1)S(1)} fusion(bf16[32,48,32,64]{3,2,1,0:T(8,128)(2,1)} %reshape.166), kind=kLoop, calls=%fused_computation.19 | loop fusion | bytes 12582912 | tf_op jit(solution)/shard_map/reshape | solution.py:13
  473.1 1.5 copy.17
  474.7 3.1 fusion
  477.8 6.1 %copy.20 = bf16[64,2,48,2,16]{4,3,2,1,0:T(2,128)(2,1)S(1)} copy(bf16[64,2,48,2,16]{0,4,3,1,2:T(8,128)(2,1)} %fusion) | data formatting | bytes 786432 | tf_op jit(solution)/shard_map/convert_element_type | solution.py:64
  483.9 2.7 copy.21
  486.5 42.3 %all_to_all.23 = bf16[128,96,16]{1,2,0:T(8,128)(2,1)S(1)} all-to-all(bf16[128,96,16]{1,2,0:T(8,128)(2,1)} %copy.21), channel_id=1, replica_groups=mesh['grp'=16,'sp'=32] {'sp'}, dimensions={0} | all-to-all | bytes 786432 | tf_op jit(solution)/shard_map/all_to_all | solution.py:66
  (22 shorter events, 3.8 us)
Async XLA Ops:
  6.5 85.6 %all-gather.2.cloned.1.call-start = ((), (), s32[]{:S(2)}) async-start(), calls=%async_computation.2 | async-start | bytes 6488064 | tf_op jit(solution)/shard_map/all_gather | solution.py:49
  102.9 2.8 copy-start
  113.3 1.6 copy-start.1
  113.3 9.7 %copy-start.3 = (f32[32]{0:T(128)S(1)}, f32[32]{0:T(128)}, u32[]{:S(2)}) copy-start(f32[32]{0:T(128)} %param.15) | copy-start | bytes 388
  114.9 11.4 %copy-start.4 = (f32[32]{0:T(128)S(1)}, f32[32]{0:T(128)}, u32[]{:S(2)}) copy-start(f32[32]{0:T(128)} %param.17) | copy-start | bytes 388
  114.9 11.4 %copy-start.5 = (f32[32]{0:T(128)S(1)}, f32[32]{0:T(128)}, u32[]{:S(2)}) copy-start(f32[32]{0:T(128)} %param.16) | copy-start | bytes 388
  159.1 8.6 %copy-start.6 = (bf16[16]{0:T(256)(128)(2,1)S(1)}, bf16[16]{0:T(256)(128)(2,1)}, u32[]{:S(2)}) copy-start(bf16[16]{0:T(256)(128)(2,1)} %param.19) | copy-start | bytes 100
  159.1 283.3 %all-to-all-start = ((bf16[32,2,49152]{2,1,0:T(2,128)(2,1)}), bf16[32,2,49152]{2,1,0:T(2,128)(2,1)}, u32[]{:S(2)}, u32[]{:S(2)}) async-start(bf16[32,2,49152]{2,1,0:T(2,128)(2,1)} %reshape.165), calls=%async_computation | async-start | bytes 12582912 | tf_op jit(solution)/shard_map/all_to_all | solution.py:12
  473.1 1.5 copy-start.2
Sparse Core Ops, SparseCore 0:
  9.5 82.6 all-gather.1
